TPU v7x, 32 devices: a whole 2x2x4 slice. The times are simulated.
32 devices in a mesh: item: 2 (over x), lat: 4 (over y, core), pix: 4 (over z).
Axes of the slice: x: 2, y: 2, z: 4, core: 2. Of those that a mesh axis runs over, the one named last changes fastest.
Arguments:
- latents: bfloat16 [8, 512, 1024], P('item', ('lat', 'pix')), may hold values from -6 to 6
- pixels: bfloat16 [8, 32768, 261], P('item', ('lat', 'pix')), may hold values from -6 to 6
- size_ids: int32 [8], P('item'), may hold values from 0 to 2, as said below
- cross_gain: float32 [1024], replicated, may hold values from 0.25 to 1.75
- pixel_gain: float32 [261], replicated, may hold values from 0.25 to 1.75
- query_weight: bfloat16 [1024, 1024], replicated, may hold values from -0.1875 to 0.1875
- key_weight: bfloat16 [261, 1024], replicated, may hold values from -0.375 to 0.375
- value_weight: bfloat16 [261, 1024], replicated, may hold values from -0.375 to 0.375
- cross_output: bfloat16 [1024, 1024], replicated, may hold values from -9 to 9
- first_gain: float32 [1024], replicated, may hold values from 0.25 to 1.75
- first_up: bfloat16 [1024, 1024], replicated, may hold values from -0.1875 to 0.1875
- first_down: bfloat16 [1024, 1024], replicated, may hold values from -0.1875 to 0.1875
- self_gain: float32 [1024], replicated, may hold values from 0.25 to 1.75
- self_inputs: bfloat16 [1024, 3072], replicated, may hold values from -0.1875 to 0.1875
- self_output: bfloat16 [1024, 1024], replicated, may hold values from -2.5 to 2.5
- second_gain: float32 [1024], replicated, may hold values from 0.25 to 1.75
- second_up: bfloat16 [1024, 1024], replicated, may hold values from -0.1875 to 0.1875
- second_down: bfloat16 [1024, 1024], replicated, may hold values from -0.1875 to 0.1875
- cotangent: bfloat16 [8, 512, 1024], P('item', ('lat', 'pix')), may hold values from -6 to 6
Outputs:
- latents_out: bfloat16 [8, 512, 1024], P('item', ('lat', 'pix'))
- latent_grad: bfloat16 [8, 512, 1024], P('item', ('lat', 'pix'))
- pixel_grad: bfloat16 [8, 32768, 261], P('item', ('lat', 'pix'))
- query_grad: float32 [1024, 1024], P(('item', 'lat', 'pix'))
- cross_out_grad: float32 [1024, 1024], P(('item', 'lat', 'pix'))
- first_up_grad: float32 [1024, 1024], P(('item', 'lat', 'pix'))
- first_down_grad: float32 [1024, 1024], P(('item', 'lat', 'pix'))
- self_in_grad: float32 [1024, 3072], P(('item', 'lat', 'pix'))
- self_out_grad: float32 [1024, 1024], P(('item', 'lat', 'pix'))
- second_up_grad: float32 [1024, 1024], P(('item', 'lat', 'pix'))
- second_down_grad: float32 [1024, 1024], P(('item', 'lat', 'pix'))
- key_grad: float32 [261, 1024], replicated
- value_grad: float32 [261, 1024], replicated
- cross_gain_grad: float32 [1024], replicated
- pixel_gain_grad: float32 [261], replicated
- first_gain_grad: float32 [1024], replicated
- self_gain_grad: float32 [1024], replicated
- second_gain_grad: float32 [1024], replicated
Inputs may be any that keep to these rules, and one draw needn't show every extreme that they name: `size_ids`: each of the sizes 0, 1 and 2 is given to at least one image.
All inputs are finite; a program needn't handle non-finite values.
Results may differ from a plain program's by a relative error of at most 0.025.
Values may be sent and summed in bfloat16 or wider, within the bound.
No kernel may reach another device: no remote copies, remote signals or barrier semaphores. Data moves between devices by JAX's collectives and lax.ppermute only.
A program may use at most 256 MiB of HBM per device.

v0:
```python
import math

import jax
import jax.numpy as jnp
from jax import lax
from jax.sharding import PartitionSpec as P

HEADS = 8


epsilon = 1e-05


def norm_rows(inputs, gain):
    centred = inputs - jnp.mean(inputs, axis=-1, keepdims=True)
    inverse = lax.rsqrt(jnp.mean(centred * centred, axis=-1, keepdims=True) + epsilon)
    normed = centred * inverse
    return (normed * gain, normed, inverse)


def norm_back(upstream, normed, inverse, gain):
    scaled = upstream * gain
    first_mean = jnp.mean(scaled, axis=-1, keepdims=True)
    second_mean = jnp.mean(scaled * normed, axis=-1, keepdims=True)
    return inverse * (scaled - first_mean - normed * second_mean)


def activation(inputs):
    return jax.nn.gelu(inputs, approximate=True)


def forward_mat(left, right):
    return jnp.dot(left, right, preferred_element_type=jnp.float32)


def left_mat(left, right):
    return jnp.einsum("rk,rd->kd", left, right, preferred_element_type=jnp.float32)


def right_mat(left, right):
    return jnp.einsum("rd,kd->rk", left, right, preferred_element_type=jnp.float32)


def feed_forward(residual, gain, up_weight, down_weight):
    normed_full, normed, inverse = norm_rows(residual, gain)
    rounded_in = normed_full.astype(jnp.bfloat16)
    hidden = forward_mat(rounded_in, up_weight)
    active = activation(hidden).astype(jnp.bfloat16)
    return (
        residual + forward_mat(active, down_weight),
        (rounded_in, normed, inverse, hidden, active),
    )


def feed_back(upstream, kept, gain, up_weight, down_weight):
    rounded_in, normed, inverse, hidden, active = kept
    sent = upstream.astype(jnp.bfloat16)
    down_grad = left_mat(active, sent)
    unused, gelu_pull = jax.vjp(activation, hidden)
    hidden_grad = gelu_pull(right_mat(sent, down_weight))[0].astype(jnp.bfloat16)
    up_grad = left_mat(rounded_in, hidden_grad)
    normed_grad = right_mat(hidden_grad, up_weight)
    gain_grad = jnp.sum(normed_grad * normed, axis=0)
    return (upstream + norm_back(normed_grad, normed, inverse, gain), up_grad, down_grad, gain_grad)


def body(
    latents,
    pixels,
    size_ids,
    cross_gain,
    pixel_gain,
    query_weight,
    key_weight,
    value_weight,
    cross_output,
    first_gain,
    first_up,
    first_down,
    self_gain,
    self_inputs,
    self_output,
    second_gain,
    second_up,
    second_down,
    cotangent,
):
    images, lat_rows, width = latents.shape
    pix_rows = pixels.shape[1]
    head_dim = width // HEADS
    group = lax.axis_size(("lat", "pix"))
    block = lax.axis_index(("lat", "pix"))
    all_rows = lat_rows * group
    rows = images * lat_rows
    scale = 1.0 / math.sqrt(width)
    head_scale = 1.0 / math.sqrt(head_dim)
    factor = jnp.where(size_ids == 0, 25, jnp.where(size_ids == 1, 49, 81)).astype(jnp.int32)
    counts = pix_rows * group * factor // 81
    positions = block * pix_rows + jnp.arange(pix_rows, dtype=jnp.int32)
    valid = positions[None, :] < counts[:, None]
    residual_zero = latents.astype(jnp.float32).reshape(rows, width)
    normed_full, normed_one, inverse_one = norm_rows(residual_zero, cross_gain)
    rounded_one = normed_full.astype(jnp.bfloat16)
    query_own = (
        forward_mat(rounded_one, query_weight).astype(jnp.bfloat16).reshape(images, lat_rows, width)
    )
    query_all = lax.all_gather(query_own, ("lat", "pix"), axis=1, tiled=True)
    pixel_full, pixel_normed, pixel_inverse = norm_rows(pixels.astype(jnp.float32), pixel_gain)
    pixel_rounded = pixel_full.astype(jnp.bfloat16)
    pixel_keys = jnp.einsum(
        "ipc,cd->ipd", pixel_rounded, key_weight, preferred_element_type=jnp.float32
    ).astype(jnp.bfloat16)
    pixel_values = jnp.einsum(
        "ipc,cd->ipd", pixel_rounded, value_weight, preferred_element_type=jnp.float32
    ).astype(jnp.bfloat16)
    scores = (
        jnp.einsum("ild,ipd->ilp", query_all, pixel_keys, preferred_element_type=jnp.float32)
        * scale
    )
    powered = jnp.where(valid[:, None, :], jnp.exp(scores), 0.0)
    powered_low = powered.astype(jnp.bfloat16)
    totals = jnp.sum(powered, axis=2)
    numerator = jnp.einsum(
        "ilp,ipd->ild", powered_low, pixel_values, preferred_element_type=jnp.float32
    )
    numer_all, totals_all = (
        lax.psum(numerator.astype(jnp.bfloat16), ("lat", "pix")).astype(jnp.float32),
        lax.psum(totals.astype(jnp.bfloat16), ("lat", "pix")).astype(jnp.float32),
    )
    start = block * lat_rows
    numer_own = lax.dynamic_slice_in_dim(numer_all, start, lat_rows, 1)
    totals_own = lax.dynamic_slice_in_dim(totals_all, start, lat_rows, 1)
    attended = numer_own / totals_own[:, :, None]
    cross_mixed = attended.astype(jnp.bfloat16).reshape(rows, width)
    residual_one = residual_zero + forward_mat(cross_mixed, cross_output)
    residual_two, first_kept = feed_forward(residual_one, first_gain, first_up, first_down)
    normed_full, normed_three, inverse_three = norm_rows(residual_two, self_gain)
    rounded_three = normed_full.astype(jnp.bfloat16)
    projected = (
        forward_mat(rounded_three, self_inputs)
        .astype(jnp.bfloat16)
        .reshape(images, lat_rows, 3 * width)
    )
    pair_all = lax.all_gather(projected[:, :, width:], ("lat", "pix"), axis=1, tiled=True)
    self_query = projected[:, :, :width].reshape(images, lat_rows, HEADS, head_dim)
    self_keys = pair_all[:, :, :width].reshape(images, all_rows, HEADS, head_dim)
    self_values = pair_all[:, :, width:].reshape(images, all_rows, HEADS, head_dim)
    self_scores = (
        jnp.einsum("ilhe,imhe->ihlm", self_query, self_keys, preferred_element_type=jnp.float32)
        * head_scale
    )
    self_powered = jnp.exp(self_scores)
    self_low = self_powered.astype(jnp.bfloat16)
    self_totals = jnp.transpose(jnp.sum(self_powered, axis=3), (0, 2, 1))
    self_numerator = jnp.einsum(
        "ihlm,imhe->ilhe", self_low, self_values, preferred_element_type=jnp.float32
    )
    self_mixed = self_numerator / self_totals[..., None]
    self_rounded = self_mixed.astype(jnp.bfloat16).reshape(rows, width)
    residual_three = residual_two + forward_mat(self_rounded, self_output)
    output_rows, second_kept = feed_forward(residual_three, second_gain, second_up, second_down)
    latents_out = output_rows.astype(jnp.bfloat16).reshape(images, lat_rows, width)
    upstream = cotangent.astype(jnp.float32).reshape(rows, width)
    back_three, second_up_grad, second_down_grad, second_gain_grad = feed_back(
        upstream, second_kept, second_gain, second_up, second_down
    )
    sent_three = back_three.astype(jnp.bfloat16)
    self_out_grad = left_mat(self_rounded, sent_three)
    mixed_grad = (
        right_mat(sent_three, self_output)
        .astype(jnp.bfloat16)
        .reshape(images, lat_rows, HEADS, head_dim)
    )
    mixed_wide = mixed_grad.astype(jnp.float32)
    numer_grad = (mixed_wide / self_totals[..., None]).astype(jnp.bfloat16)
    total_grad = -jnp.sum(mixed_wide * self_mixed, axis=3) / self_totals
    power_grad = jnp.einsum(
        "ilhe,imhe->ihlm", numer_grad, self_values, preferred_element_type=jnp.float32
    )
    score_grad = (
        self_powered * (power_grad + jnp.transpose(total_grad, (0, 2, 1))[..., None])
    ).astype(jnp.bfloat16)
    query_part = (
        jnp.einsum("ihlm,imhe->ilhe", score_grad, self_keys, preferred_element_type=jnp.float32)
        * head_scale
    )
    key_part = (
        jnp.einsum("ihlm,ilhe->imhe", score_grad, self_query, preferred_element_type=jnp.float32)
        * head_scale
    )
    value_part = jnp.einsum(
        "ihlm,ilhe->imhe", self_low, numer_grad, preferred_element_type=jnp.float32
    )
    pair_grad = jnp.concatenate(
        [key_part.reshape(images, all_rows, width), value_part.reshape(images, all_rows, width)],
        axis=2,
    )
    pair_own = lax.psum_scatter(
        pair_grad.astype(jnp.bfloat16), ("lat", "pix"), scatter_dimension=1, tiled=True
    ).astype(jnp.float32)
    projected_grad = (
        jnp.concatenate([query_part.reshape(images, lat_rows, width), pair_own], axis=2)
        .astype(jnp.bfloat16)
        .reshape(rows, 3 * width)
    )
    self_in_grad = left_mat(rounded_three, projected_grad)
    normed_grad = right_mat(projected_grad, self_inputs)
    self_gain_grad = jnp.sum(normed_grad * normed_three, axis=0)
    back_two = back_three + norm_back(normed_grad, normed_three, inverse_three, self_gain)
    back_one, first_up_grad, first_down_grad, first_gain_grad = feed_back(
        back_two, first_kept, first_gain, first_up, first_down
    )
    sent_one = back_one.astype(jnp.bfloat16)
    cross_out_grad = left_mat(cross_mixed, sent_one)
    attended_grad = right_mat(sent_one, cross_output).astype(jnp.bfloat16).astype(jnp.float32)
    attended_grad = attended_grad.reshape(images, lat_rows, width)
    numer_own_grad = (attended_grad / totals_own[:, :, None]).astype(jnp.bfloat16)
    totals_own_grad = -jnp.sum(attended_grad * attended, axis=2) / totals_own
    numer_grad_all, totals_grad_all = (
        lax.all_gather(numer_own_grad, ("lat", "pix"), axis=1, tiled=True),
        lax.all_gather(
            totals_own_grad.astype(jnp.bfloat16), ("lat", "pix"), axis=1, tiled=True
        ).astype(totals_own_grad.dtype),
    )
    cross_power_grad = jnp.einsum(
        "ild,ipd->ilp", numer_grad_all, pixel_values, preferred_element_type=jnp.float32
    )
    cross_score_grad = (powered * (cross_power_grad + totals_grad_all[:, :, None])).astype(
        jnp.bfloat16
    )
    query_part_cross = (
        jnp.einsum("ilp,ipd->ild", cross_score_grad, pixel_keys, preferred_element_type=jnp.float32)
        * scale
    )
    query_rows_grad = lax.psum_scatter(
        query_part_cross.astype(jnp.bfloat16), ("lat", "pix"), scatter_dimension=1, tiled=True
    ).astype(jnp.float32)
    query_rows_grad = query_rows_grad.astype(jnp.bfloat16).reshape(rows, width)
    key_rows_grad = (
        jnp.einsum("ilp,ild->ipd", cross_score_grad, query_all, preferred_element_type=jnp.float32)
        * scale
    ).astype(jnp.bfloat16)
    value_rows_grad = jnp.einsum(
        "ilp,ild->ipd", powered_low, numer_grad_all, preferred_element_type=jnp.float32
    ).astype(jnp.bfloat16)
    pixel_normed_grad = jnp.einsum(
        "ipd,cd->ipc", key_rows_grad, key_weight, preferred_element_type=jnp.float32
    ) + jnp.einsum("ipd,cd->ipc", value_rows_grad, value_weight, preferred_element_type=jnp.float32)
    key_grad = jnp.einsum(
        "ipc,ipd->cd", pixel_rounded, key_rows_grad, preferred_element_type=jnp.float32
    )
    value_grad = jnp.einsum(
        "ipc,ipd->cd", pixel_rounded, value_rows_grad, preferred_element_type=jnp.float32
    )
    pixel_gain_grad = jnp.sum(pixel_normed_grad * pixel_normed, axis=(0, 1))
    pixel_grad = norm_back(pixel_normed_grad, pixel_normed, pixel_inverse, pixel_gain).astype(
        jnp.bfloat16
    )
    query_grad = left_mat(rounded_one, query_rows_grad)
    normed_one_grad = right_mat(query_rows_grad, query_weight)
    cross_gain_grad = jnp.sum(normed_one_grad * normed_one, axis=0)
    latent_grad = back_one + norm_back(normed_one_grad, normed_one, inverse_one, cross_gain)
    latent_grad = latent_grad.astype(jnp.bfloat16).reshape(images, lat_rows, width)
    (
        query_grad,
        cross_out_grad,
        first_up_grad,
        first_down_grad,
        self_in_grad,
        self_out_grad,
        second_up_grad,
        second_down_grad,
    ) = (
        lax.psum_scatter(query_grad, ("item", "lat", "pix"), scatter_dimension=0, tiled=True),
        lax.psum_scatter(cross_out_grad, ("item", "lat", "pix"), scatter_dimension=0, tiled=True),
        lax.psum_scatter(first_up_grad, ("item", "lat", "pix"), scatter_dimension=0, tiled=True),
        lax.psum_scatter(first_down_grad, ("item", "lat", "pix"), scatter_dimension=0, tiled=True),
        lax.psum_scatter(self_in_grad, ("item", "lat", "pix"), scatter_dimension=0, tiled=True),
        lax.psum_scatter(self_out_grad, ("item", "lat", "pix"), scatter_dimension=0, tiled=True),
        lax.psum_scatter(second_up_grad, ("item", "lat", "pix"), scatter_dimension=0, tiled=True),
        lax.psum_scatter(second_down_grad, ("item", "lat", "pix"), scatter_dimension=0, tiled=True),
    )
    (
        key_grad,
        value_grad,
        cross_gain_grad,
        pixel_gain_grad,
        first_gain_grad,
        self_gain_grad,
        second_gain_grad,
    ) = lax.psum(
        (
            key_grad,
            value_grad,
            cross_gain_grad,
            pixel_gain_grad,
            first_gain_grad,
            self_gain_grad,
            second_gain_grad,
        ),
        ("item", "lat", "pix"),
    )
    return (
        latents_out,
        latent_grad,
        pixel_grad,
        query_grad,
        cross_out_grad,
        first_up_grad,
        first_down_grad,
        self_in_grad,
        self_out_grad,
        second_up_grad,
        second_down_grad,
        key_grad,
        value_grad,
        cross_gain_grad,
        pixel_gain_grad,
        first_gain_grad,
        self_gain_grad,
        second_gain_grad,
    )


def solution(mesh):
    in_specs = (
        P("item", ("lat", "pix"), None),
        P("item", ("lat", "pix"), None),
        P("item"),
        P(),
        P(),
        P(),
        P(),
        P(),
        P(),
        P(),
        P(),
        P(),
        P(),
        P(),
        P(),
        P(),
        P(),
        P(),
        P("item", ("lat", "pix"), None),
    )
    out_specs = (
        P("item", ("lat", "pix"), None),
        P("item", ("lat", "pix"), None),
        P("item", ("lat", "pix"), None),
        P(("item", "lat", "pix"), None),
        P(("item", "lat", "pix"), None),
        P(("item", "lat", "pix"), None),
        P(("item", "lat", "pix"), None),
        P(("item", "lat", "pix"), None),
        P(("item", "lat", "pix"), None),
        P(("item", "lat", "pix"), None),
        P(("item", "lat", "pix"), None),
        P(),
        P(),
        P(),
        P(),
        P(),
        P(),
        P(),
    )
    return jax.shard_map(body, mesh=mesh, in_specs=in_specs, out_specs=out_specs, check_vma=False)
```

profile of v0, /device:TPU:0, one launch (start us, length us, event | category | flops | bytes accessed | tf_op | source)
XLA Modules:
  0.0 2006.8 jit_solution(15135687993326305070)
XLA Ops:
  22.3 20.6 %convolution_convert_fusion.1 = bf16[4,2048,1024]{2,1,0:T(8,128)(2,1)} fusion(bf16[261,1024]{1,0:T(8,128)(2,1)S(1)} %copy-done.60, f32[261]{0:T(512)S(1)} %copy-done.56, f32[4,2048]{1,0:T(4,128)S(1)} %add_rsqrt_fusion, f32[4,2048]{1,0:T(4,128)S(1)} %broadcast_multiply_fusion.2, bf16[4,2048,261]{1,0,2:T(4,128)(2,1)S(1)} %copy-done.3), kind=kOutput, calls=%fused_computation.4 | convolution fusion | flops 4397932544 | bytes 21654548 | tf_op jit(solution)/shard_map/ipc,cd->ipd/dot_general | solution.py:113
  42.9 20.6 %convolution_convert_fusion.2 = bf16[4,2048,1024]{2,1,0:T(8,128)(2,1)} fusion(bf16[261,1024]{1,0:T(8,128)(2,1)S(1)} %copy-done.58, f32[261]{0:T(512)S(1)} %copy-done.56, f32[4,2048]{1,0:T(4,128)S(1)} %add_rsqrt_fusion, f32[4,2048]{1,0:T(4,128)S(1)} %broadcast_multiply_fusion.2, bf16[4,2048,261]{1,0,2:T(4,128)(2,1)S(1)} %copy-done.3), kind=kOutput, calls=%fused_computation.5 | convolution fusion | flops 4397932544 | bytes 21654548 | tf_op jit(solution)/shard_map/ipc,cd->ipd/dot_general | solution.py:110
  67.1 18.3 fusion
  85.4 18.5 convolution_convert_fusion.5
  104.0 32.8 %psum.64 = bf16[4,512]{1,0:T(4,128)(2,1)S(1)} all-reduce(bf16[4,512]{1,0:T(4,128)(2,1)S(1)} %get-tuple-element.116), channel_id=1, replica_groups=mesh['item'=2,'lat'=4,'pix'=4] {'lat','pix'}, use_global_device_ids=true, to_apply=%region_6.7 | all-reduce | flops 2048 | bytes 8192 | tf_op jit(solution)/shard_map/psum | solution.py:128
  136.9 78.2 %all-reduce.5.cloned.1.call-done = bf16[4,512,1024]{2,1,0:T(8,128)(2,1)} async-done(((bf16[4,512,1024]{2,1,0:T(8,128)(2,1)}), bf16[4,512,1024]{2,1,0:T(8,128)(2,1)}) %all-reduce.5.cloned.1.call-update) | async-done | bytes 4194320 | tf_op jit(solution)/shard_map/psum | solution.py:127
  229.7 70.3 %all-gather.7.cloned.1.call-done = bf16[4,512,2048]{2,0,1:T(4,128)(2,1)} async-done(((bf16[4,32,2048]{2,0,1:T(4,128)(2,1)}), bf16[4,512,2048]{2,0,1:T(4,128)(2,1)}) %all-gather.7.cloned.1.call-update) | async-done | bytes 8388624 | tf_op jit(solution)/shard_map/all_gather | solution.py:144
  299.9 8.3 fusion.91
  308.2 7.5 copy.107
  320.1 7.5 copy.106
  359.4 8.2 pad_maximum_fusion
  371.7 98.1 %reduce-scatter.11.cloned.1.call-done = bf16[4,32,2048]{2,1,0:T(8,128)(2,1)} async-done(((bf16[4,512,2048]{2,1,0:T(8,128)(2,1)}), bf16[4,32,2048]{2,1,0:T(8,128)(2,1)}) %reduce-scatter.11.cloned.1.call-update) | async-done | bytes 524304 | tf_op jit(solution)/shard_map/reduce_scatter | solution.py:198
  481.9 31.2 %all-gather = bf16[16,32,4]{1,2,0:T(4,128)(2,1)S(1)} all-gather(bf16[1,32,4]{1,2,0:T(4,128)(2,1)S(1)} %fusion.74), channel_id=1, replica_groups=mesh['item'=2,'lat'=4,'pix'=4] {'lat','pix'}, dimensions={0}, use_global_device_ids=true | all-gather | bytes 4352 | tf_op jit(solution)/shard_map/all_gather | solution.py:221
  513.2 19.0 all-gather.9.cloned.1.call-done
  532.2 16.2 multiply_convert_fusion.1
  551.6 13.7 multiply_convert_fusion.2
  585.1 13.2 convolution_convert_fusion
  604.0 11.7 convolution_bitcast_fusion.1
  615.7 16.0 multiply_convert_fusion
  631.7 16.3 convolution_bitcast_fusion.2
  662.2 19.6 fusion.25
  681.9 17.8 fusion.13
  712.6 41.0 %all-reduce = (f32[1024]{0:T(1024)}, f32[261]{0:T(512)}, f32[1024]{0:T(1024)}, f32[1024]{0:T(1024)}, f32[1024]{0:T(1024)}) all-reduce(f32[1024]{0:T(1024)S(1)} %get-tuple-element.99, f32[261]{0:T(512)S(1)} %get-tuple-element.90, f32[1024]{0:T(1024)S(1)} %get-tuple-element.97, ...), channel_id=1, replica_groups=mesh['item'=2,'lat'=4,'pix'=4] {'item','lat','pix'}, use_global_device_ids=true, to_apply=%region_39.40 | all-reduce | flops 4357 | bytes 34856 | tf_op jit(solution)/shard_map/psum | solution.py:291
  754.5 34.3 %reduce-scatter.27.cloned.1.call-done = f32[32,1024]{1,0:T(8,128)} async-done(((f32[1024,1024]{1,0:T(8,128)}), f32[32,1024]{1,0:T(8,128)}) %reduce-scatter.27.cloned.1.call-update) | async-done | bytes 131088 | tf_op jit(solution)/shard_map/reduce_scatter | solution.py:280
  788.8 151.1 %reduce-scatter.25.cloned.1.call-done = f32[32,1024]{1,0:T(8,128)} async-done(((f32[1024,1024]{1,0:T(8,128)}), f32[32,1024]{1,0:T(8,128)}) %reduce-scatter.25.cloned.1.call-update) | async-done | bytes 131088 | tf_op jit(solution)/shard_map/reduce_scatter | solution.py:279
  939.9 151.1 %reduce-scatter.29.cloned.1.call-done = f32[32,1024]{1,0:T(8,128)} async-done(((f32[1024,1024]{1,0:T(8,128)}), f32[32,1024]{1,0:T(8,128)}) %reduce-scatter.29.cloned.1.call-update) | async-done | bytes 131088 | tf_op jit(solution)/shard_map/reduce_scatter | solution.py:281
  1091.0 150.5 %reduce-scatter.21.cloned.1.call-done = f32[32,1024]{1,0:T(8,128)} async-done(((f32[1024,1024]{1,0:T(8,128)}), f32[32,1024]{1,0:T(8,128)}) %reduce-scatter.21.cloned.1.call-update) | async-done | bytes 131088 | tf_op jit(solution)/shard_map/reduce_scatter | solution.py:277
  1241.5 150.9 %reduce-scatter.19.cloned.1.call-done = f32[32,1024]{1,0:T(8,128)} async-done(((f32[1024,1024]{1,0:T(8,128)}), f32[32,1024]{1,0:T(8,128)}) %reduce-scatter.19.cloned.1.call-update) | async-done | bytes 131088 | tf_op jit(solution)/shard_map/reduce_scatter | solution.py:276
  1392.4 151.4 %reduce-scatter.17.cloned.1.call-done = f32[32,1024]{1,0:T(8,128)} async-done(((f32[1024,1024]{1,0:T(8,128)}), f32[32,1024]{1,0:T(8,128)}) %reduce-scatter.17.cloned.1.call-update) | async-done | bytes 131088 | tf_op jit(solution)/shard_map/reduce_scatter | solution.py:275
  1543.8 140.2 %all-reduce.7.cloned.1.call-done = (f32[261,1024]{1,0:T(8,128)}, f32[261,1024]{1,0:T(8,128)}) async-done(((f32[261,1024]{1,0:T(8,128)}, f32[261,1024]{1,0:T(8,128)}), (f32[261,1024]{1,0:T(8,128)}, f32[261,1024]{1,0:T(8,128)})) %all-reduce.7.cloned.1.call-update) | async-done | bytes 2138128 | tf_op jit(solution)/shard_map/psum | solution.py:291
  1684.0 160.5 %reduce-scatter.23.cloned.1.call-done = f32[32,3072]{1,0:T(8,128)} async-done(((f32[1024,3072]{1,0:T(8,128)}), f32[32,3072]{1,0:T(8,128)}) %reduce-scatter.23.cloned.1.call-update) | async-done | bytes 393232 | tf_op jit(solution)/shard_map/reduce_scatter | solution.py:278
  1844.5 150.6 %reduce-scatter.15.cloned.1.call-done = f32[32,1024]{1,0:T(8,128)} async-done(((f32[1024,1024]{1,0:T(8,128)}), f32[32,1024]{1,0:T(8,128)}) %reduce-scatter.15.cloned.1.call-update) | async-done | bytes 131088 | tf_op jit(solution)/shard_map/reduce_scatter | solution.py:274
  (253 shorter events, 146.2 us)
Async XLA Ops:
  7.2 325.8 %copy-start = (bf16[1024,1024]{1,0:T(8,128)(2,1)S(1)}, bf16[1024,1024]{1,0:T(8,128)(2,1)}, u32[]{:S(2)}) copy-start(bf16[1024,1024]{1,0:T(8,128)(2,1)} %param.35) | copy-start | bytes 6291460
  7.2 59.9 %all-gather.5.cloned.1.call-start = ((), (), s32[]{:S(2)}) async-start(), calls=%async_computation.10 | async-start | bytes 4456448 | tf_op jit(solution)/shard_map/all_gather | solution.py:107
  13.8 201.3 %all-reduce.5.cloned.1.call-start = ((), (), s32[]{:S(2)}) async-start(), calls=%async_computation.11 | async-start | bytes 8388608 | tf_op jit(solution)/shard_map/psum | solution.py:127
  19.8 23.1 %copy-start.39 = (f32[4,2048]{1,0:T(4,128)}, f32[4,2048]{1,0:T(4,128)S(1)}, u32[]{:S(2)}) copy-start(f32[4,2048]{1,0:T(4,128)S(1)} %broadcast_multiply_fusion.2) | copy-start | bytes 98308
  22.2 20.6 %copy-start.42 = (f32[4,2048]{1,0:T(4,128)}, f32[4,2048]{1,0:T(4,128)S(1)}, u32[]{:S(2)}) copy-start(f32[4,2048]{1,0:T(4,128)S(1)} %add_rsqrt_fusion) | copy-start | bytes 98308
  22.3 20.6 %copy-start.58 = (bf16[261,1024]{1,0:T(8,128)(2,1)S(1)}, bf16[261,1024]{1,0:T(8,128)(2,1)}, u32[]{:S(2)}) copy-start(bf16[261,1024]{1,0:T(8,128)(2,1)} %param.25) | copy-start | bytes 1603588
  103.9 112.5 %copy-start.15 = (bf16[4,32,1024]{2,1,0:T(8,128)(2,1)S(1)}, bf16[4,32,1024]{2,1,0:T(8,128)(2,1)}, u32[]{:S(2)}) copy-start(bf16[4,32,1024]{2,1,0:T(8,128)(2,1)} %param.19) | copy-start | bytes 786436
  103.9 115.0 %copy-start.44 = (f32[1024]{0:T(1024)S(1)}, f32[1024]{0:T(1024)}, u32[]{:S(2)}) copy-start(f32[1024]{0:T(1024)} %param.28) | copy-start | bytes 12292
  103.9 196.0 %all-gather.7.cloned.1.call-start = ((), (), s32[]{:S(2)}) async-start(), calls=%async_computation.12 | async-start | bytes 8912896 | tf_op jit(solution)/shard_map/all_gather | solution.py:144
  226.3 243.4 %reduce-scatter.11.cloned.1.call-start = ((), (), s32[]{:S(2)}) async-start(), calls=%async_computation.13 | async-start | bytes 8912896 | tf_op jit(solution)/shard_map/reduce_scatter | solution.py:198
  367.6 164.6 %all-gather.9.cloned.1.call-start = ((), (), s32[]{:S(2)}) async-start(), calls=%async_computation.14 | async-start | bytes 4456448 | tf_op jit(solution)/shard_map/all_gather | solution.py:220
  371.7 98.1 %copy-start.35 = (bf16[16,8,8,128]{3,1,2,0:T(8,128)(2,1)}, bf16[16,8,8,128]{3,1,2,0:T(8,128)(2,1)S(1)}, u32[]{:S(2)}) copy-start(bf16[16,8,8,128]{3,1,2,0:T(8,128)(2,1)S(1)} %copy.148) | copy-start | bytes 786436
  479.0 103.3 %copy-start.7 = (f32[128,1024]{1,0:T(8,128)}, f32[128,1024]{1,0:T(8,128)S(1)}, u32[]{:S(2)}) copy-start(f32[128,1024]{1,0:T(8,128)S(1)} %multiply_add_fusion) | copy-start | bytes 1572868
  481.8 172.9 %reduce-scatter.13.cloned.1.call-start = ((), (), s32[]{:S(2)}) async-start(), calls=%async_computation.15 | async-start | bytes 4456448 | tf_op jit(solution)/shard_map/reduce_scatter | solution.py:235
  565.3 223.4 %reduce-scatter.27.cloned.1.call-start = ((), (), s32[]{:S(2)}) async-start(), calls=%async_computation.22 | async-start | bytes 4325376 | tf_op jit(solution)/shard_map/reduce_scatter | solution.py:280
  569.2 370.7 %reduce-scatter.25.cloned.1.call-start = ((), (), s32[]{:S(2)}) async-start(), calls=%async_computation.21 | async-start | bytes 4325376 | tf_op jit(solution)/shard_map/reduce_scatter | solution.py:279
  572.5 518.5 %reduce-scatter.29.cloned.1.call-start = ((), (), s32[]{:S(2)}) async-start(), calls=%async_computation.23 | async-start | bytes 4325376 | tf_op jit(solution)/shard_map/reduce_scatter | solution.py:281
  576.5 665.0 %reduce-scatter.21.cloned.1.call-start = ((), (), s32[]{:S(2)}) async-start(), calls=%async_computation.19 | async-start | bytes 4325376 | tf_op jit(solution)/shard_map/reduce_scatter | solution.py:277
  579.4 813.0 %reduce-scatter.19.cloned.1.call-start = ((), (), s32[]{:S(2)}) async-start(), calls=%async_computation.18 | async-start | bytes 4325376 | tf_op jit(solution)/shard_map/reduce_scatter | solution.py:276
  582.2 961.6 %reduce-scatter.17.cloned.1.call-start = ((), (), s32[]{:S(2)}) async-start(), calls=%async_computation.17 | async-start | bytes 4325376 | tf_op jit(solution)/shard_map/reduce_scatter | solution.py:275
  585.0 19.0 copy-start.40
  585.0 19.0 copy-start.43
  585.1 19.0 copy-start.57
  585.1 1098.9 %all-reduce.7.cloned.1.call-start = ((), (), s32[]{:S(2)}) async-start(), calls=%async_computation.24 | async-start | bytes 4325376 | tf_op jit(solution)/shard_map/psum | solution.py:291
  631.7 16.4 copy-start.37
  648.1 1196.4 %reduce-scatter.23.cloned.1.call-start = ((), (), s32[]{:S(2)}) async-start(), calls=%async_computation.20 | async-start | bytes 12976128 | tf_op jit(solution)/shard_map/reduce_scatter | solution.py:278
  654.6 1340.6 %reduce-scatter.15.cloned.1.call-start = ((), (), s32[]{:S(2)}) async-start(), calls=%async_computation.16 | async-start | bytes 4325376 | tf_op jit(solution)/shard_map/reduce_scatter | solution.py:274
  659.3 22.6 %slice-start = ((s8[4276224]{0:T(1024)(128)(4,1)}), s8[81920]{0:T(1024)(128)(4,1)S(1)}, s32[]{:S(2)}) async-start(s8[4276224]{0:T(1024)(128)(4,1)} %bitcast.147), calls=%async_computation.25 | async-start | bytes 163840
  662.2 19.6 slice-start.1
  662.2 19.6 copy-start.61
  706.2 47.3 %copy-start.8 = (f32[128,1024]{1,0:T(8,128)S(1)}, f32[128,1024]{1,0:T(8,128)}, u32[]{:S(2)}) copy-start(f32[128,1024]{1,0:T(8,128)} %copy-done.7) | copy-start | bytes 1572868
  711.6 1288.3 %copy-start.1 = (bf16[1024,1024]{1,0:T(8,128)(2,1)S(1)}, bf16[1024,1024]{1,0:T(8,128)(2,1)}, u32[]{:S(2)}) copy-start(bf16[1024,1024]{1,0:T(8,128)(2,1)} %param.35) | copy-start | bytes 6291460
  (50 other events, 235.5 us)
Sparse Core Ops, SparseCore 0:
  13.9 53.1 all-gather.4
  104.0 111.0 all-reduce.4
  226.5 73.4 all-gather.6
  367.7 102.0 reduce-scatter.10
  481.9 50.2 all-gather.8
  565.4 71.2 reduce-scatter.12
  639.6 149.1 reduce-scatter.26
  791.6 148.2 reduce-scatter.24
  942.7 148.2 reduce-scatter.28
  1093.7 147.7 reduce-scatter.20
  1244.4 147.9 reduce-scatter.18
  1395.1 148.6 reduce-scatter.16
  1550.1 133.8 all-reduce.6
  1690.5 154.0 reduce-scatter.22
  1847.2 147.8 reduce-scatter.14
where the time goes:
time: 2010 us
  waiting for transfers between devices  1510 us (75%)
  matrix products  282 us (14%)
  blocking collectives  105 us (5%)
  local copies, waits for them, and re-layouts  59.6 us (3%)
  other arithmetic  33.4 us (2%)
    reduce_scatter x1, waiting for transfers between devices, body(): lax.psum_scatter(self_in_grad, ('item', 'lat', 'pix'), scatter_dimension=...  161 us
    reduce_scatter x1, waiting for transfers between devices, body(): lax.psum_scatter(cross_out_grad, ('item', 'lat', 'pix'), scatter_dimensio...  151 us
    reduce_scatter x1, waiting for transfers between devices, body(): lax.psum_scatter(second_down_grad, ('item', 'lat', 'pix'), scatter_dimens...  151 us
    reduce_scatter x1, waiting for transfers between devices, body(): lax.psum_scatter(self_out_grad, ('item', 'lat', 'pix'), scatter_dimension...  151 us
    reduce_scatter x1, waiting for transfers between devices, body(): lax.psum_scatter(first_up_grad, ('item', 'lat', 'pix'), scatter_dimension...  151 us
    reduce_scatter x1, waiting for transfers between devices, body(): lax.psum_scatter(query_grad, ('item', 'lat', 'pix'), scatter_dimension=0,...  151 us
    reduce_scatter x1, waiting for transfers between devices, body(): lax.psum_scatter(first_down_grad, ('item', 'lat', 'pix'), scatter_dimensi...  151 us
    psum x1, waiting for transfers between devices, body(): lax.psum((key_grad, value_grad, cross_gain_grad, pixel_gain_grad, first_g...  140 us
  transfers between devices with their start and end apart: 15, of which 14 were waited for; matrix products, arithmetic and copies ran while one was open for 10% of the time, Pallas kernels for 0%

commit v1 on v0

v1 whole, which is shorter than its diff:
```python
import math
from functools import partial

import jax
import jax.numpy as jnp
from jax import lax
from jax.experimental import pallas as pl
from jax.experimental.pallas import tpu as pltpu
from jax.sharding import Mesh, PartitionSpec as P

HEADS = 8
LANES = 128
epsilon = 1e-05
f32 = jnp.float32
bf16 = jnp.bfloat16

NN = (((1,), (0,)), ((), ()))
NT = (((1,), (1,)), ((), ()))
TN = (((0,), (0,)), ((), ()))


def dot(left, right, dims=NN):
    return lax.dot_general(left, right, dims, preferred_element_type=f32)


def norm_rows(inputs, gain):
    centred = inputs - jnp.mean(inputs, axis=-1, keepdims=True)
    inverse = lax.rsqrt(jnp.mean(centred * centred, axis=-1, keepdims=True) + epsilon)
    normed = centred * inverse
    return (normed * gain, normed, inverse)


def norm_back(upstream, normed, inverse, gain):
    scaled = upstream * gain
    first_mean = jnp.mean(scaled, axis=-1, keepdims=True)
    second_mean = jnp.mean(scaled * normed, axis=-1, keepdims=True)
    return inverse * (scaled - first_mean - normed * second_mean)


def activation(inputs):
    return jax.nn.gelu(inputs, approximate=True)


def pixel_norm(x_ref, channels):
    raw = x_ref[0].astype(f32)
    rows, padded = raw.shape
    lane = lax.broadcasted_iota(jnp.int32, (rows, padded), 1)
    inside = lane < channels
    raw = jnp.where(inside, raw, 0.0)
    mean = jnp.sum(raw, axis=1, keepdims=True) * (1.0 / channels)
    centred = jnp.where(inside, raw - mean, 0.0)
    inverse = lax.rsqrt(
        jnp.sum(centred * centred, axis=1, keepdims=True) * (1.0 / channels) + epsilon
    )
    return centred * inverse, inverse, lane, inside


def rounded_pixels(normed, gain, lane, channels):
    ones = jnp.where((lane >= channels) & (lane < channels + 2), 1.0, 0.0)
    return (normed * gain + ones).astype(bf16)


def both_halves(a_ref, b_ref, padded):
    rows = math.prod(a_ref.shape) // padded
    return jnp.concatenate(
        [a_ref[...].reshape(rows, padded), b_ref[...].reshape(rows, padded)], axis=0
    )


def cross_forward_kernel(
    counts_ref, x_ref, gain_ref, qa_ref, qb_ref, p_ref, na_ref, nb_ref, acc_ref, *, channels, tile
):
    image, step = pl.program_id(0), pl.program_id(1)
    padded = x_ref.shape[2]

    @pl.when(step == 0)
    def _():
        acc_ref[...] = jnp.zeros_like(acc_ref)

    left = counts_ref[image] - step * tile

    @pl.when(left > 0)
    def _():
        normed, _, lane, _ = pixel_norm(x_ref, channels)
        pixels = rounded_pixels(normed, gain_ref[...], lane, channels)
        queries = both_halves(qa_ref, qb_ref, padded)
        scores = dot(pixels, queries, NT)
        row = lax.broadcasted_iota(jnp.int32, scores.shape, 0)
        powered = jnp.where(row < left, jnp.exp(scores), 0.0).astype(bf16)
        p_ref[0] = powered
        acc_ref[...] += dot(powered, pixels, TN)

    @pl.when(step == pl.num_programs(1) - 1)
    def _():
        half = acc_ref.shape[0] // 2
        na_ref[...] = acc_ref[:half].reshape(na_ref.shape).astype(bf16)
        nb_ref[...] = acc_ref[half:].reshape(nb_ref.shape).astype(bf16)


def cross_backward_kernel(
    counts_ref,
    x_ref,
    gain_ref,
    qa_ref,
    qb_ref,
    ga_ref,
    gb_ref,
    p_ref,
    out_ref,
    ta_ref,
    tb_ref,
    acc_ref,
    *,
    channels,
    tile,
):
    image, step = pl.program_id(0), pl.program_id(1)
    padded = x_ref.shape[2]

    @pl.when(step == 0)
    def _():
        acc_ref[...] = jnp.zeros_like(acc_ref)

    left = counts_ref[image] - step * tile

    @pl.when(left > 0)
    def _():
        gain = gain_ref[...]
        normed, inverse, lane, inside = pixel_norm(x_ref, channels)
        pixels = rounded_pixels(normed, gain, lane, channels)
        queries = both_halves(qa_ref, qb_ref, padded)
        grads = both_halves(ga_ref, gb_ref, padded)
        powered = p_ref[0]
        power_grad = dot(pixels, grads, NT)
        score_grad = (powered.astype(f32) * power_grad).astype(bf16)
        acc_ref[...] += dot(score_grad, pixels, TN)
        upstream = dot(score_grad, queries) + dot(powered, grads)
        scaled = jnp.where(inside, upstream * gain, 0.0)
        first_mean = jnp.sum(scaled, axis=1, keepdims=True) * (1.0 / channels)
        second_mean = jnp.sum(scaled * normed, axis=1, keepdims=True) * (1.0 / channels)
        out_ref[0] = (inverse * (scaled - first_mean - normed * second_mean)).astype(bf16)

    @pl.when(left <= 0)
    def _():
        out_ref[...] = jnp.zeros_like(out_ref)

    @pl.when(step == pl.num_programs(1) - 1)
    def _():
        half = acc_ref.shape[0] // 2
        ta_ref[...] = acc_ref[:half].reshape(ta_ref.shape).astype(bf16)
        tb_ref[...] = acc_ref[half:].reshape(tb_ref.shape).astype(bf16)


def cross_specs(images, pix_rows, padded, tile, fine, share):
    pixel = pl.BlockSpec((1, tile, padded), lambda i, s, c: (i, s, 0))
    gain = pl.BlockSpec((1, padded), lambda i, s, c: (0, 0))
    outer, rows = fine
    latent = pl.BlockSpec((outer, 1, rows, padded), lambda i, s, c: (0, i, 0, 0))
    gathered = pl.BlockSpec((outer, 1, rows, padded), lambda i, s, c: (0, i, 0, 0))
    shared = pl.BlockSpec((share[0], 1, share[1], padded), lambda i, s, c: (0, i, 0, 0))
    return pixel, gain, latent, gathered, shared


PIXEL_TILE = 512


def cross_forward(counts, pixels, gain, qa, qb, image_rows):
    images, pix_rows, channels = pixels.shape
    sources, _, rows, padded = qa.shape
    latents = 2 * sources * rows
    tile = min(PIXEL_TILE, pix_rows)
    steps = pix_rows // tile
    outer = sources * rows // image_rows
    query = pl.BlockSpec((sources, 1, rows, padded), lambda i, s, c: (0, i, 0, 0))
    numer = pl.BlockSpec((outer, 1, image_rows, padded), lambda i, s, c: (0, i, 0, 0))
    numer_shape = jax.ShapeDtypeStruct((outer, images, image_rows, padded), bf16)
    flops = 2 * 2 * images * latents * pix_rows * padded
    return pl.pallas_call(
        partial(cross_forward_kernel, channels=channels, tile=tile),
        grid_spec=pltpu.PrefetchScalarGridSpec(
            num_scalar_prefetch=1,
            grid=(images, steps),
            in_specs=[
                pl.BlockSpec((1, tile, padded), lambda i, s, c: (i, s, 0)),
                pl.BlockSpec((1, padded), lambda i, s, c: (0, 0)),
                query,
                query,
            ],
            out_specs=[
                pl.BlockSpec((1, tile, latents), lambda i, s, c: (i, s, 0)),
                numer,
                numer,
            ],
            scratch_shapes=[pltpu.VMEM((latents, padded), f32)],
        ),
        out_shape=[
            jax.ShapeDtypeStruct((images, pix_rows, latents), bf16),
            numer_shape,
            numer_shape,
        ],
        compiler_params=pltpu.CompilerParams(dimension_semantics=("arbitrary", "arbitrary")),
        cost_estimate=pl.CostEstimate(
            flops=flops,
            bytes_accessed=2 * images * pix_rows * (padded + latents),
            transcendentals=images * pix_rows * latents,
        ),
        name="cross_forward",
    )(counts, pixels, gain, qa, qb)


def cross_backward(counts, pixels, gain, qa, qb, ga, gb, powered):
    images, pix_rows, channels = pixels.shape
    sources, _, rows, padded = qa.shape
    outer, _, image_rows, _ = ga.shape
    latents = 2 * sources * rows
    tile = min(PIXEL_TILE, pix_rows)
    steps = pix_rows // tile
    query = pl.BlockSpec((sources, 1, rows, padded), lambda i, s, c: (0, i, 0, 0))
    grad = pl.BlockSpec((outer, 1, image_rows, padded), lambda i, s, c: (0, i, 0, 0))
    pixel = pl.BlockSpec((1, tile, padded), lambda i, s, c: (i, s, 0))
    t_shape = jax.ShapeDtypeStruct((sources, images, rows, padded), bf16)
    flops = 2 * 4 * images * latents * pix_rows * padded
    return pl.pallas_call(
        partial(cross_backward_kernel, channels=channels, tile=tile),
        grid_spec=pltpu.PrefetchScalarGridSpec(
            num_scalar_prefetch=1,
            grid=(images, steps),
            in_specs=[
                pixel,
                pl.BlockSpec((1, padded), lambda i, s, c: (0, 0)),
                query,
                query,
                grad,
                grad,
                pl.BlockSpec((1, tile, latents), lambda i, s, c: (i, s, 0)),
            ],
            out_specs=[pixel, query, query],
            scratch_shapes=[pltpu.VMEM((latents, padded), f32)],
        ),
        out_shape=[jax.ShapeDtypeStruct(pixels.shape, bf16), t_shape, t_shape],
        compiler_params=pltpu.CompilerParams(dimension_semantics=("arbitrary", "arbitrary")),
        cost_estimate=pl.CostEstimate(
            flops=flops,
            bytes_accessed=2 * images * pix_rows * (2 * padded + latents),
            transcendentals=0,
        ),
        name="cross_backward",
    )(counts, pixels, gain, qa, qb, ga, gb, powered)


def self_forward_kernel(q_ref, kv_refs, out_ref, *, head_scale):
    width = q_ref.shape[1]
    dim = width // HEADS
    for head in range(HEADS):
        cut = slice(head * dim, (head + 1) * dim)
        over = slice(width + head * dim, width + (head + 1) * dim)
        query = q_ref[:, cut]
        keys = jnp.concatenate([ref[:, cut] for ref in kv_refs], axis=0)
        values = jnp.concatenate([ref[:, over] for ref in kv_refs], axis=0)
        powered = jnp.exp(dot(query, keys, NT) * head_scale)
        totals = jnp.sum(powered, axis=1, keepdims=True)
        out_ref[:, cut] = (dot(powered.astype(bf16), values) / totals).astype(bf16)


def self_forward(query, parts, head_scale):
    count = len(parts)

    def kernel(*refs):
        self_forward_kernel(refs[0], refs[1 : 1 + count], refs[1 + count], head_scale=head_scale)

    return pl.pallas_call(
        kernel, out_shape=jax.ShapeDtypeStruct(query.shape, bf16), name="self_forward"
    )(query, *parts)


def self_backward_kernel(q_ref, g_ref, kv_refs, dq_ref, dkv_refs, *, head_scale):
    rows, width = q_ref.shape
    dim = width // HEADS
    for head in range(HEADS):
        cut = slice(head * dim, (head + 1) * dim)
        over = slice(width + head * dim, width + (head + 1) * dim)
        query = q_ref[:, cut]
        upstream = g_ref[:, cut].astype(f32)
        keys = jnp.concatenate([ref[:, cut] for ref in kv_refs], axis=0)
        values = jnp.concatenate([ref[:, over] for ref in kv_refs], axis=0)
        powered = jnp.exp(dot(query, keys, NT) * head_scale)
        low = powered.astype(bf16)
        totals = jnp.sum(powered, axis=1, keepdims=True)
        mixed = dot(low, values) / totals
        numer_grad = (upstream / totals).astype(bf16)
        total_grad = -jnp.sum(upstream * mixed, axis=1, keepdims=True) / totals
        score_grad = (powered * (dot(numer_grad, values, NT) + total_grad)).astype(bf16)
        dq_ref[:, cut] = (dot(score_grad, keys) * head_scale).astype(bf16)
        key_grad = (dot(score_grad, query, TN) * head_scale).astype(bf16)
        value_grad = dot(low, numer_grad, TN).astype(bf16)
        for at, ref in enumerate(dkv_refs):
            ref[:, cut] = key_grad[at * rows : (at + 1) * rows]
            ref[:, over] = value_grad[at * rows : (at + 1) * rows]


def self_backward(query, upstream, parts, head_scale):
    count = len(parts)

    def kernel(*refs):
        self_backward_kernel(
            refs[0],
            refs[1],
            refs[2 : 2 + count],
            refs[2 + count],
            refs[3 + count :],
            head_scale=head_scale,
        )

    return pl.pallas_call(
        kernel,
        out_shape=[jax.ShapeDtypeStruct(query.shape, bf16)]
        + [jax.ShapeDtypeStruct(part.shape, bf16) for part in parts],
        name="self_backward",
    )(query, upstream, *parts)


def swap(value, axis):
    return lax.ppermute(value, axis, [(0, 1), (1, 0)])


def pix_exchange(value):
    size = lax.axis_size("pix")
    me = lax.axis_index("pix")
    out = value
    for step in range(1, size):
        perm = [(at, at ^ step) for at in range(size)]
        peer = me ^ step
        got = lax.ppermute(lax.dynamic_index_in_dim(value, peer, 0, keepdims=True), "pix", perm)
        out = lax.dynamic_update_slice_in_dim(out, got, peer, 0)
    return out


GRID = ("laty", "pix")
EVERY = ("item", "laty", "pix")


def spread(value, axes):
    size = lax.axis_size(axes)
    many = jnp.broadcast_to(value[None], (size,) + value.shape)
    return lax.all_to_all(many, axes, split_axis=0, concat_axis=0, tiled=True)


def pair_sum(mine, theirs):
    return (mine.astype(f32) + swap(theirs, "latc").astype(f32)).astype(bf16)


def collect(value, axes):
    got = lax.all_to_all(value, axes, split_axis=0, concat_axis=0, tiled=True)
    size = lax.axis_size(axes)
    got = got.reshape((size, value.shape[0] // size) + value.shape[1:])
    return jnp.sum(got.astype(f32), axis=0)


def body(
    latents,
    pixels,
    size_ids,
    cross_gain,
    pixel_gain,
    query_weight,
    key_weight,
    value_weight,
    cross_output,
    first_gain,
    first_up,
    first_down,
    self_gain,
    self_inputs,
    self_output,
    second_gain,
    second_up,
    second_down,
    cotangent,
):
    images, lat_rows, width = latents.shape
    pix_rows, channels = pixels.shape[1:]
    padded = -(-(channels + 2) // LANES) * LANES
    head_scale = 1.0 / math.sqrt(width // HEADS)
    scale = 1.0 / math.sqrt(width)
    items, laty, latc, pix = (lax.axis_size(a) for a in ("item", "laty", "latc", "pix"))
    assert images == pix and latc == 2 and laty == 2
    group = laty * latc * pix
    grid = laty * pix
    rows = images * lat_rows
    core = lax.axis_index("latc")
    block = lax.axis_index(("laty", "latc", "pix"))
    factor = jnp.where(size_ids == 0, 25, jnp.where(size_ids == 1, 49, 81)).astype(jnp.int32)
    counts = pix_rows * group * factor // 81
    counts = jnp.clip(counts - block * pix_rows, 0, pix_rows)
    lanes = ((0, padded - channels),)
    key_pad = jnp.pad(key_weight, lanes + ((0, 0),))
    value_pad = jnp.pad(value_weight, lanes + ((0, 0),))
    gain_pad = jnp.pad(pixel_gain, lanes)[None]

    latents_here = latents.astype(f32).reshape(rows, width)
    normed_full, normed_one, inverse_one = norm_rows(latents_here, cross_gain)
    rounded_one = normed_full.astype(bf16)
    query_rows = dot(rounded_one, query_weight).astype(bf16)
    query_low = (dot(query_rows, key_pad, NT) * scale).astype(bf16)
    qa = spread(query_low.reshape(images, lat_rows, padded), GRID)
    qb = swap(qa, "latc")
    powered, numer_a, numer_b = cross_forward(counts, pixels, gain_pad, qa, qb, pix * lat_rows)

    residual_zero = pix_exchange(latents).astype(f32).reshape(rows, width)
    upstream = pix_exchange(cotangent).reshape(rows, width)
    numer = collect(
        pair_sum(numer_a, numer_b).reshape(grid, rows, padded), GRID
    ).reshape(rows, padded)
    totals = numer[:, channels : channels + 1]
    numer_mean = (numer / totals).astype(bf16)
    attended = dot(numer_mean, value_pad)
    cross_mixed = attended.astype(bf16)
    residual_one = residual_zero + dot(cross_mixed, cross_output)

    def feed_forward(residual, gain, up_weight, down_weight):
        normed_full, normed, inverse = norm_rows(residual, gain)
        rounded_in = normed_full.astype(bf16)
        hidden = dot(rounded_in, up_weight)
        active = activation(hidden).astype(bf16)
        return residual + dot(active, down_weight), (rounded_in, normed, inverse, hidden, active)

    def shared_left(left):
        parts = left.reshape(rows, items * laty, 2, -1)
        mine = lax.dynamic_index_in_dim(parts, core, 2, keepdims=False)
        theirs = lax.dynamic_index_in_dim(parts, 1 - core, 2, keepdims=False)
        return jnp.concatenate([mine, swap(theirs, "latc")], axis=0).reshape(2 * rows, -1)

    def shared_right(right):
        return jnp.concatenate([right, swap(right, "latc")], axis=0)

    def weight_grad(left, right):
        grad = dot(shared_left(left), shared_right(right), TN).astype(bf16)
        return grad.reshape(items * grid, -1, right.shape[1])

    def scatter(grads):
        whole = jnp.concatenate(grads, axis=2)
        for axis in EVERY:
            whole = lax.psum_scatter(whole, axis, scatter_dimension=0, tiled=True)
        whole = whole[0].astype(f32)
        out, at = [], 0
        for grad in grads:
            out.append(whole[:, at : at + grad.shape[2]])
            at += grad.shape[2]
        return out

    residual_two, first_kept = feed_forward(residual_one, first_gain, first_up, first_down)
    normed_full, normed_three, inverse_three = norm_rows(residual_two, self_gain)
    rounded_three = normed_full.astype(bf16)
    projected = dot(rounded_three, self_inputs).astype(bf16)
    self_query = projected[:, :width]
    pair = projected[:, width:]
    pair_y = swap(pair, "laty")
    parts = (pair, pair_y, swap(pair, "latc"), swap(pair_y, "latc"))
    self_rounded = self_forward(self_query, parts, head_scale)
    residual_three = residual_two + dot(self_rounded, self_output)
    output_rows, second_kept = feed_forward(residual_three, second_gain, second_up, second_down)
    latents_out = pix_exchange(output_rows.astype(bf16).reshape(images, lat_rows, width))

    def feed_back(upstream, kept, gain, up_weight, down_weight):
        rounded_in, normed, inverse, hidden, active = kept
        sent = upstream.astype(bf16)
        down_grad = weight_grad(active, sent)
        _, gelu_pull = jax.vjp(activation, hidden)
        hidden_grad = gelu_pull(dot(sent, down_weight, NT))[0].astype(bf16)
        up_grad = weight_grad(rounded_in, hidden_grad)
        normed_grad = dot(hidden_grad, up_weight, NT)
        gain_grad = jnp.sum(normed_grad * normed, axis=0)
        return (
            upstream.astype(f32) + norm_back(normed_grad, normed, inverse, gain),
            up_grad,
            down_grad,
            gain_grad,
        )

    back_three, second_up_part, second_down_part, second_gain_part = feed_back(
        upstream, second_kept, second_gain, second_up, second_down
    )
    sent_three = back_three.astype(bf16)
    self_out_part = weight_grad(self_rounded, sent_three)
    second_up_grad, second_down_grad, self_out_grad = scatter(
        [second_up_part, second_down_part, self_out_part]
    )
    mixed_grad = dot(sent_three, self_output, NT).astype(bf16)
    query_part, own, at_y, at_c, at_yc = self_backward(self_query, mixed_grad, parts, head_scale)
    near = pair_sum(own, at_c)
    far = pair_sum(at_y, at_yc)
    pair_own = (near.astype(f32) + swap(far, "laty").astype(f32)).astype(bf16)
    projected_grad = jnp.concatenate([query_part, pair_own], axis=1)
    self_in_part = weight_grad(rounded_three, projected_grad)
    normed_grad = dot(projected_grad, self_inputs, NT)
    self_gain_part = jnp.sum(normed_grad * normed_three, axis=0)
    back_two = back_three + norm_back(normed_grad, normed_three, inverse_three, self_gain)
    back_one, first_up_part, first_down_part, first_gain_part = feed_back(
        back_two, first_kept, first_gain, first_up, first_down
    )
    self_in_grad, first_up_grad, first_down_grad = scatter(
        [self_in_part, first_up_part, first_down_part]
    )
    sent_one = back_one.astype(bf16)
    attended_grad = dot(sent_one, cross_output, NT).astype(bf16).astype(f32)
    numer_grad = (attended_grad / totals).astype(bf16)
    total_grad = -jnp.sum(attended_grad * attended, axis=1, keepdims=True) / totals
    lane = lax.broadcasted_iota(jnp.int32, (rows, padded), 1)
    high = total_grad.astype(bf16).astype(f32)
    grad_low = dot(numer_grad, value_pad, NT)
    grad_low = jnp.where(lane == channels, high, grad_low)
    grad_low = jnp.where(lane == channels + 1, total_grad - high, grad_low).astype(bf16)
    ga = spread(grad_low, GRID).reshape(laty, images, rows, padded)
    gb = swap(ga, "latc")
    pixel_grad, t_a, t_b = cross_backward(counts, pixels, gain_pad, qa, qb, ga, gb, powered)
    back_here = pix_exchange(sent_one.reshape(images, lat_rows, width))
    t_rows = collect(pair_sum(t_a, t_b), GRID).reshape(rows, padded)
    t_low = (t_rows * scale).astype(bf16)
    query_rows_grad = dot(t_low, key_pad).astype(bf16)
    normed_one_grad = dot(query_rows_grad, query_weight, NT)
    latent_grad = back_here.astype(f32).reshape(rows, width) + norm_back(
        normed_one_grad, normed_one, inverse_one, cross_gain
    )
    latent_grad = latent_grad.astype(bf16).reshape(images, lat_rows, width)

    first_sum = dot(rounded_one, t_low, TN)
    second_sum = dot(sent_one, numer_mean, TN)
    wide = lax.broadcasted_iota(jnp.int32, (width, padded), 1)
    for at, part in enumerate((first_gain_part, self_gain_part, second_gain_part)):
        column = channels + 2 * at
        part = part[:, None]
        high = part.astype(bf16).astype(f32)
        first_sum = jnp.where(wide == column, high, first_sum)
        first_sum = jnp.where(wide == column + 1, part - high, first_sum)
    sums = jnp.stack([first_sum, second_sum]).astype(bf16)
    sums = sums.reshape(2, items, laty, 2, pix, -1, padded).transpose(3, 1, 2, 4, 0, 5, 6)
    sums = sums.reshape((2, items * grid) + sums.shape[4:])
    mine = lax.dynamic_index_in_dim(sums, core, 0, keepdims=False)
    theirs = lax.dynamic_index_in_dim(sums, 1 - core, 0, keepdims=False)
    owned = collect(pair_sum(mine, theirs), EVERY)[0].astype(bf16)
    mine = spread(owned, EVERY)
    theirs = swap(mine, "latc")
    low = jnp.where(core == 0, mine, theirs)
    high = jnp.where(core == 0, theirs, mine)
    sums = jnp.stack([low, high]).reshape((2, items, laty, pix) + owned.shape)
    sums = sums.transpose(4, 1, 2, 0, 3, 5, 6).reshape(2, width, padded)
    first_sum, second_sum = sums[0], sums[1]
    gains = [
        first_sum[:, channels + 2 * at].astype(f32) + first_sum[:, channels + 2 * at + 1].astype(f32)
        for at in range(3)
    ]
    first_gain_grad, self_gain_grad, second_gain_grad = gains
    clean = jnp.where(wide < channels, first_sum, 0).astype(bf16)
    query_grad = dot(owned[0], key_pad)
    key_grad = dot(clean, query_weight, TN)[:channels]
    weights = dot(query_weight, key_pad, NT)
    cross_gain_grad = jnp.sum(clean.astype(f32) * weights, axis=1) / cross_gain
    value_grad = dot(second_sum, cross_output, (((0,), (1,)), ((), ())))[:channels]
    start = (lax.axis_index(("item", "laty", "latc", "pix"))) * owned.shape[1]
    columns = lax.dynamic_slice_in_dim(value_pad, start, owned.shape[1], 1)
    cross_out_grad = dot(columns, second_sum, (((0,), (1,)), ((), ())))
    pixel_gain_grad = (
        jnp.sum(
            key_grad * key_weight.astype(f32) + value_grad * value_weight.astype(f32), axis=1
        )
        / pixel_gain
    )
    return (
        latents_out,
        latent_grad,
        pixel_grad,
        query_grad,
        cross_out_grad,
        first_up_grad,
        first_down_grad,
        self_in_grad,
        self_out_grad,
        second_up_grad,
        second_down_grad,
        key_grad,
        value_grad,
        cross_gain_grad,
        pixel_gain_grad,
        first_gain_grad,
        self_gain_grad,
        second_gain_grad,
    )


def solution(mesh):
    items, lat, pix = (mesh.shape[name] for name in ("item", "lat", "pix"))
    fine = Mesh(
        mesh.devices.reshape(items, lat // 2, 2, pix), ("item", "laty", "latc", "pix")
    )
    group = ("laty", "latc", "pix")
    rows = P("item", group, None)
    split = P(("item",) + group, None)
    in_specs = (rows, rows, P("item")) + (P(),) * 15 + (rows,)
    out_specs = (rows, rows, rows) + (split,) * 8 + (P(),) * 7
    return jax.shard_map(
        body, mesh=fine, in_specs=in_specs, out_specs=out_specs, check_vma=False
    )
```

time: 2010 us -> 519 us (0.26)
  waiting for transfers between devices: 1510 us -> 144 us
  matrix products: 282 us -> 60.9 us
  Pallas kernels: 0 us -> 66.3 us
  blocking collectives: 105 us -> 54.1 us
  starting transfers between devices: 1.31 us -> 45.2 us
  local copies, waits for them, and re-layouts: 59.6 us -> 87.6 us
    reduce_scatter x10 -> x6, waiting for transfers between devices: 1200 us -> 29.3 us  [scatter(): whole = lax.psum_scatter(whole, axis, scatter_dimension=0, tiled=True)]
    dot_general x42 -> x31, matrix products: 282 us -> 60.9 us  [dot(): return lax.dot_general(left, right, dims, preferred_element_type=f32)]
    psum x2 -> x0, waiting for transfers between devices: 218 us -> none  [the longest x1 140 us: body(): lax.psum((key_grad, value_grad, cross_gain_grad, pixel_gain_grad, first_g...]
    all_gather x3 -> x0, waiting for transfers between devices: 92.8 us -> none  [the longest x1 70.3 us: body(): lax.all_gather(projected[:, :, width:], ('lat', 'pix'), axis=1, tiled=True)]
    psum x2 -> x0, blocking collectives: 73.8 us -> none  [the longest x1 41 us: body(): lax.psum((key_grad, value_grad, cross_gain_grad, pixel_gain_grad, first_g...]
    ppermute x0 -> x36, waiting for transfers between devices: none -> 71.9 us  [the longest x12 47.3 us: pix_exchange(): lax.ppermute(lax.dynamic_index_in_dim(value, peer, 0, keepdims=True), 'pi...]
    pallas_call x0 -> x4, Pallas kernels: none -> 66.3 us  [the longest x1 33.1 us: cross_backward(): pl.pallas_call(partial(cross_backward_kernel, channels=channels, tile=til...]
    all_to_all x0 -> x2, blocking collectives: none -> 54.1 us  [spread(): return lax.all_to_all(many, axes, split_axis=0, concat_axis=0, tiled=True)]
  transfers between devices with their start and end apart: 15 -> 46, of which waited for: 14 -> 21; matrix products, arithmetic and copies ran while one was open for 10% -> 31% of each run, Pallas kernels for 0% -> 9%
where the time goes in v1:
time: 519 us; the launch traced here: 512 us
  waiting for transfers between devices  144 us (28%)
  local copies, waits for them, and re-layouts  87.6 us (17%)
  Pallas kernels  66.3 us (13%)
  matrix products  60.9 us (12%)
  blocking collectives  54.1 us (10%)
  starting transfers between devices  45.2 us (9%)
  other arithmetic  38.1 us (7%)
  between operations  16 us (3%)
    dot_general x31, matrix products, dot(): return lax.dot_general(left, right, dims, preferred_element_type=f32)  60.9 us
    all_to_all x2, blocking collectives, spread(): return lax.all_to_all(many, axes, split_axis=0, concat_axis=0, tiled=True)  54.1 us
    ppermute x12, waiting for transfers between devices, pix_exchange(): lax.ppermute(lax.dynamic_index_in_dim(value, peer, 0, keepdims=True), 'pi...  47.3 us
    all_to_all x3, waiting for transfers between devices, collect(): got = lax.all_to_all(value, axes, split_axis=0, concat_axis=0, tiled=True)  42.3 us
    unnamed x171, local copies, waits for them, and re-layouts  41.2 us
    pallas_call x1, Pallas kernels, cross_backward(): pl.pallas_call(partial(cross_backward_kernel, channels=channels, tile=til...  33.1 us
    reduce_scatter x6, waiting for transfers between devices, scatter(): whole = lax.psum_scatter(whole, axis, scatter_dimension=0, tiled=True)  29.3 us
    ppermute x24, waiting for transfers between devices, swap(): return lax.ppermute(value, axis, [(0, 1), (1, 0)])  24.6 us
  transfers between devices with their start and end apart: 46, of which 21 were waited for; matrix products, arithmetic and copies ran while one was open for 31% of the time, Pallas kernels for 9%

profile of v1, /device:TPU:0, one launch (start us, length us, event | category | flops | bytes accessed | tf_op | source)
XLA Modules:
  0.0 512.1 jit_solution(3535956175102869116)
XLA Ops:
  16.2 28.1 %all_to_all.30.qa_ref = bf16[8,4,32,384]{3,2,1,0:T(8,128)(2,1)S(1)} all-to-all(bf16[8,4,32,384]{3,2,1,0:T(8,128)(2,1)S(1)} %broadcast_in_dim.121), channel_id=1, replica_groups=mesh['item'=2,'laty'=2,'latc'=2,'pix'=4] {'laty','pix'}, dimensions={0} | all-to-all | bytes 1572864 | tf_op jit(solution)/shard_map/all_to_all | solution.py:345
  44.3 10.8 %copy.115.x_ref = bf16[4,2048,261]{2,1,0:T(8,128)(2,1)} copy(bf16[4,2048,261]{1,0,2:T(4,128)(2,1)} %param.20) | data formatting | bytes 8552448 | tf_op args[1]
  56.2 22.0 %cross_forward.1 = (bf16[4,2048,512]{2,1,0:T(8,128)(2,1)}, bf16[2,4,128,384]{3,2,1,0:T(8,128)(2,1)}, bf16[2,4,128,384]{3,2,1,0:T(8,128)(2,1)}) custom-call(s32[4]{0:T(128)} %subtract_clamp_fusion.counts_ref, bf16[4,2048,261]{2,1,0:T(8,128)(2,1)} %copy.115.x_ref, f32[1,384]{1,0:T(1,128)} %broadcast_in_dim.119.gain_ref, bf16[8,4,32,384]{3,2,1,0:T(8,128)(2,1)} %copy-done.37, ...), custom_call_target="tpu_custom_call" | custom-call | flops 6442450944 | bytes 14680064 | tf_op jit(solution)/shard_map/cross_forward/pallas_call | solution.py:178
  82.9 3.5 all-to-all-start.1
  88.7 13.3 %collective-permute-done = bf16[1,32,1024]{2,1,0:T(8,128)(2,1)S(1)} collective-permute-done((bf16[1,32,1024]{2,1,0:T(8,128)(2,1)S(1)}, bf16[1,32,1024]{2,1,0:T(8,128)(2,1)S(1)}, u32[]{:S(2)}, u32[]{:S(2)}) %collective-permute-start) | collective-permute-done | bytes 65568 | tf_op jit(solution)/shard_map/ppermute | solution.py:333
  102.0 3.9 collective-permute-start.1
  106.9 4.5 collective-permute-done.1
  121.4 10.6 %collective-permute-done.5.refs_2_.refs_3_ = bf16[128,2048]{1,0:T(8,128)(2,1)} collective-permute-done((bf16[128,2048]{1,0:T(8,128)(2,1)S(1)}, bf16[128,2048]{1,0:T(8,128)(2,1)}, u32[]{:S(2)}, u32[]{:S(2)}) %collective-permute-start.5) | collective-permute-done | bytes 524320 | tf_op jit(solution)/shard_map/ppermute | solution.py:323
  134.3 3.1 collective-permute-done.11
  138.9 3.4 collective-permute-start.12
  142.7 3.4 collective-permute-done.12
  152.5 4.0 self_forward.1
  165.8 2.9 fusion.46
  202.0 3.2 convolution_convert_fusion.9.refs_1_
  205.3 7.3 %self_backward.1 = (bf16[128,1024]{1,0:T(8,128)(2,1)}, bf16[128,2048]{1,0:T(8,128)(2,1)}, bf16[128,2048]{1,0:T(8,128)(2,1)}, bf16[128,2048]{1,0:T(8,128)(2,1)}, bf16[128,2048]{1,0:T(8,128)(2,1)}) custom-call(bf16[128,1024]{1,0:T(8,128)(2,1)} %slice.85.refs_0_, bf16[128,1024]{1,0:T(8,128)(2,1)} %convolution_convert_fusion.9.refs_1_, ...), custom_call_target="tpu_custom_call" | custom-call | tf_op jit(solution)/shard_map/self_backward/pallas_call | solution.py:314
  233.5 5.8 %multiply_reduce_fusion.1 = (f32[1024]{0:T(1024)}, f32[128]{0:T(128)S(1)}, f32[128]{0:T(128)S(1)}, f32[128,1024]{1,0:T(8,128)S(1)}) fusion(f32[128,1024]{1,0:T(8,128)S(1)} %copy-done.2, f32[128]{0:T(128)S(1)} %copy-done.73, f32[128]{0:T(128)S(1)} %copy-done.69, f32[1024]{0:T(1024)S(1)} %copy-done.52, bf16[1024,3072]{1,0:T(8,128)(2,1)} %param.32, ...), kind=kOutput, calls=%fused_computation.113 | convolution fusion | flops 807926528 | bytes 8136704 | tf_op jit(solution)/shard_map/dot_general | solution.py:23
  260.7 2.8 pad_maximum_fusion
  271.8 26.0 %all_to_all.31 = bf16[8,128,384]{2,1,0:T(8,128)(2,1)} all-to-all(bf16[8,128,384]{2,1,0:T(8,128)(2,1)S(1)} %broadcast_in_dim.126), channel_id=1, replica_groups=mesh['item'=2,'laty'=2,'latc'=2,'pix'=4] {'laty','pix'}, dimensions={0} | all-to-all | bytes 1572864 | tf_op jit(solution)/shard_map/all_to_all | solution.py:345
  300.4 33.1 %cross_backward.1 = (bf16[4,2048,261]{2,1,0:T(8,128)(2,1)}, bf16[8,4,32,384]{3,2,1,0:T(8,128)(2,1)}, bf16[8,4,32,384]{3,2,1,0:T(8,128)(2,1)}) custom-call(s32[4]{0:T(128)} %subtract_clamp_fusion.counts_ref, bf16[4,2048,261]{2,1,0:T(8,128)(2,1)} %copy.115.x_ref, f32[1,384]{1,0:T(1,128)} %broadcast_in_dim.119.gain_ref, bf16[8,4,32,384]{3,2,1,0:T(8,128)(2,1)} %copy-done.37, ...), custom_call_target="tpu_custom_call" | custom-call | flops 12884901888 | bytes 20971520 | tf_op jit(solution)/shard_map/cross_backward/pallas_call | solution.py:223
  338.4 4.3 all-to-all-start.3
  344.6 19.7 %all-to-all-done.3 = bf16[8,4,32,384]{3,2,1,0:T(8,128)(2,1)} async-done(((bf16[8,4,32,384]{3,2,1,0:T(8,128)(2,1)}), bf16[8,4,32,384]{3,2,1,0:T(8,128)(2,1)}, u32[]{:S(2)}, u32[]{:S(2)}) %all-to-all-start.3) | async-done | bytes 786464 | tf_op jit(solution)/shard_map/all_to_all | solution.py:353
  371.4 4.3 all-to-all-start.4
  375.7 22.5 %all-to-all-done.4 = bf16[16,2,32,384]{3,2,1,0:T(8,128)(2,1)} async-done(((bf16[16,2,32,384]{3,2,1,0:T(8,128)(2,1)}), bf16[16,2,32,384]{3,2,1,0:T(8,128)(2,1)}, u32[]{:S(2)}, u32[]{:S(2)}) %all-to-all-start.4) | async-done | bytes 786464 | tf_op jit(solution)/shard_map/all_to_all | solution.py:353
  400.5 4.3 all-to-all-start.5
  408.8 9.8 %collective-permute-done.8 = bf16[1,32,1024]{2,1,0:T(8,128)(2,1)S(1)} collective-permute-done((bf16[1,32,1024]{2,1,0:T(8,128)(2,1)S(1)}, bf16[1,32,1024]{2,1,0:T(8,128)(2,1)S(1)}, u32[]{:S(2)}, u32[]{:S(2)}) %collective-permute-start.8) | collective-permute-done | bytes 65568 | tf_op jit(solution)/shard_map/ppermute | solution.py:333
  418.7 4.1 collective-permute-start.9
  423.4 4.8 collective-permute-done.9
  431.1 3.2 collective-permute-done.18
  436.4 10.9 %copy.141 = bf16[4,2048,261]{1,0,2:T(4,128)(2,1)} copy(bf16[4,2048,261]{2,1,0:T(8,128)(2,1)} %get-tuple-element.114) | data formatting | bytes 8552448
  447.5 3.4 fusion.112
  461.6 2.8 fusion.6
  473.3 29.2 %reduce-scatter.11.cloned.1.call-done = bf16[1,32,5120]{2,1,0:T(8,128)(2,1)} async-done(((bf16[4,32,5120]{2,1,0:T(8,128)(2,1)}), bf16[1,32,5120]{2,1,0:T(8,128)(2,1)}) %reduce-scatter.11.cloned.1.call-update) | async-done | bytes 327696 | tf_op jit(solution)/shard_map/reduce_scatter | solution.py:443
  (390 shorter events, 181.2 us)
Async XLA Ops:
  44.3 11.9 %collective-permute-start.3 = (bf16[8,4,32,384]{3,2,1,0:T(8,128)(2,1)S(1)}, bf16[8,4,32,384]{3,2,1,0:T(8,128)(2,1)}, u32[]{:S(2)}, u32[]{:S(2)}) collective-permute-start(bf16[8,4,32,384]{3,2,1,0:T(8,128)(2,1)S(1)} %all_to_all.30.qa_ref), channel_id=1, source_target_pairs={{0,4},{4,0},{1,5},{5,1},{2,6},{6,2},{3,7},{7,3},{8,12},{12,8},{9,1... | collective-permute-start | bytes 2359304 | tf_op jit(solution)/shard_map/ppermute | solution.py:323
  82.9 29.2 %all-to-all-start.1 = ((bf16[8,128,384]{2,1,0:T(8,128)(2,1)}), bf16[8,128,384]{2,1,0:T(8,128)(2,1)S(1)}, u32[]{:S(2)}, u32[]{:S(2)}) async-start(bf16[8,128,384]{2,1,0:T(8,128)(2,1)} %bitcast.153), calls=%async_computation.1 | async-start | bytes 1572864 | tf_op jit(solution)/shard_map/all_to_all | solution.py:353
  86.5 211.4 %reduce-scatter.13.cloned.1.call-start = ((), (), s32[]{:S(2)}) async-start(), calls=%async_computation.15 | async-start | bytes 4718592 | tf_op jit(solution)/shard_map/reduce_scatter | solution.py:443
  86.7 15.2 %collective-permute-start = (bf16[1,32,1024]{2,1,0:T(8,128)(2,1)S(1)}, bf16[1,32,1024]{2,1,0:T(8,128)(2,1)S(1)}, u32[]{:S(2)}, u32[]{:S(2)}) collective-permute-start(bf16[1,32,1024]{2,1,0:T(8,128)(2,1)S(1)} %constant_dynamic-slice_fusion.23), channel_id=1, source_target_pairs={{0,1},{1,0},{2,3},{3,2},{4,5},{5,4},{6,7},{7,6},{8,9},{9,8},{10,11... | collective-permute-start | bytes 196616 | tf_op jit(solution)/shard_map/ppermute | solution.py:333
  102.0 9.4 %collective-permute-start.1 = (bf16[1,32,1024]{2,1,0:T(8,128)(2,1)S(1)}, bf16[1,32,1024]{2,1,0:T(8,128)(2,1)S(1)}, u32[]{:S(2)}, u32[]{:S(2)}) collective-permute-start(bf16[1,32,1024]{2,1,0:T(8,128)(2,1)S(1)} %get-tuple-element.183), channel_id=1, source_target_pairs={{0,2},{1,3},{2,0},{3,1},{4,6},{5,7},{6,4},{7,5},{8,10},{9,11},{10,... | collective-permute-start | bytes 196616 | tf_op jit(solution)/shard_map/ppermute | solution.py:333
  119.9 12.1 %collective-permute-start.5 = (bf16[128,2048]{1,0:T(8,128)(2,1)S(1)}, bf16[128,2048]{1,0:T(8,128)(2,1)}, u32[]{:S(2)}, u32[]{:S(2)}) collective-permute-start(bf16[128,2048]{1,0:T(8,128)(2,1)S(1)} %slice.86.refs_1_.refs_2_), channel_id=1, source_target_pairs={{0,8},{8,0},{1,9},{9,1},{2,10},{10,2},{3,11},{11,3},{4,12},{12,4},... | collective-permute-start | bytes 1572872 | tf_op jit(solution)/shard_map/ppermute | solution.py:323
  121.4 31.1 %collective-permute-start.6 = (bf16[128,2048]{1,0:T(8,128)(2,1)S(1)}, bf16[128,2048]{1,0:T(8,128)(2,1)}, u32[]{:S(2)}, u32[]{:S(2)}) collective-permute-start(bf16[128,2048]{1,0:T(8,128)(2,1)S(1)} %slice.86.refs_1_.refs_2_), channel_id=1, source_target_pairs={{0,4},{4,0},{1,5},{5,1},{2,6},{6,2},{3,7},{7,3},{8,12},{12,8},{9,1... | collective-permute-start | bytes 1572872 | tf_op jit(solution)/shard_map/ppermute | solution.py:323
  132.0 20.5 %collective-permute-start.7 = (bf16[128,2048]{1,0:T(8,128)(2,1)}, bf16[128,2048]{1,0:T(8,128)(2,1)}, u32[]{:S(2)}, u32[]{:S(2)}) collective-permute-start(bf16[128,2048]{1,0:T(8,128)(2,1)} %collective-permute-done.5.refs_2_.refs_3_), channel_id=1, source_target_pairs={{0,4},{4,0},{1,5},{5,1},{2,6},{6,2},{3,7},{7,3},{8,12},{12,8},{9,1... | collective-permute-start | bytes 1572872 | tf_op jit(solution)/shard_map/ppermute | solution.py:323
  149.1 46.4 %collective-permute-start.33 = (bf16[128,1024]{1,0:T(8,128)(2,1)}, bf16[128,1024]{1,0:T(8,128)(2,1)}, u32[]{:S(2)}, u32[]{:S(2)}) collective-permute-start(bf16[128,1024]{1,0:T(8,128)(2,1)} %bitcast.5), channel_id=1, source_target_pairs={{0,4},{4,0},{1,5},{5,1},{2,6},{6,2},{3,7},{7,3},{8,12},{12,8},{9,1... | collective-permute-start | bytes 786440 | tf_op jit(solution)/shard_map/ppermute | solution.py:323
  172.8 16.9 %collective-permute-start.34 = (bf16[128,4,128]{2,0,1:T(8,128)(2,1)S(1)}, bf16[128,4,128]{2,0,1:T(8,128)(2,1)}, u32[]{:S(2)}, u32[]{:S(2)}) collective-permute-start(bf16[128,4,128]{2,0,1:T(8,128)(2,1)S(1)} %bitcast.171), channel_id=1, source_target_pairs={{0,4},{4,0},{1,5},{5,1},{2,6},{6,2},{3,7},{7,3},{8,12},{12,8},{9,1... | collective-permute-start | bytes 393224 | tf_op jit(solution)/shard_map/ppermute | solution.py:323
  178.2 13.9 %collective-permute-start.32 = (bf16[128,4,128]{2,0,1:T(8,128)(2,1)}, bf16[128,4,128]{2,0,1:T(8,128)(2,1)}, u32[]{:S(2)}, u32[]{:S(2)}) collective-permute-start(bf16[128,4,128]{2,0,1:T(8,128)(2,1)} %bitcast.138), channel_id=1, source_target_pairs={{0,4},{4,0},{1,5},{5,1},{2,6},{6,2},{3,7},{7,3},{8,12},{12,8},{9,1... | collective-permute-start | bytes 393224 | tf_op jit(solution)/shard_map/ppermute | solution.py:323
  181.2 12.6 %collective-permute-start.30 = (bf16[128,4,128]{2,0,1:T(8,128)(2,1)}, bf16[128,4,128]{2,0,1:T(8,128)(2,1)}, u32[]{:S(2)}, u32[]{:S(2)}) collective-permute-start(bf16[128,4,128]{2,0,1:T(8,128)(2,1)} %bitcast.139), channel_id=1, source_target_pairs={{0,4},{4,0},{1,5},{5,1},{2,6},{6,2},{3,7},{7,3},{8,12},{12,8},{9,1... | collective-permute-start | bytes 393224 | tf_op jit(solution)/shard_map/ppermute | solution.py:323
  184.5 12.6 %collective-permute-start.35 = (bf16[128,1024]{1,0:T(8,128)(2,1)}, bf16[128,1024]{1,0:T(8,128)(2,1)}, u32[]{:S(2)}, u32[]{:S(2)}) collective-permute-start(bf16[128,1024]{1,0:T(8,128)(2,1)} %get-tuple-element.148), channel_id=1, source_target_pairs={{0,4},{4,0},{1,5},{5,1},{2,6},{6,2},{3,7},{7,3},{8,12},{12,8},{9,1... | collective-permute-start | bytes 786440 | tf_op jit(solution)/shard_map/ppermute | solution.py:323
  189.7 9.0 %collective-permute-start.31 = (bf16[128,1024]{1,0:T(8,128)(2,1)}, bf16[128,1024]{1,0:T(8,128)(2,1)}, u32[]{:S(2)}, u32[]{:S(2)}) collective-permute-start(bf16[128,1024]{1,0:T(8,128)(2,1)} %copy-done.39), channel_id=1, source_target_pairs={{0,4},{4,0},{1,5},{5,1},{2,6},{6,2},{3,7},{7,3},{8,12},{12,8},{9,1... | collective-permute-start | bytes 786440 | tf_op jit(solution)/shard_map/ppermute | solution.py:323
  202.0 140.9 %reduce-scatter.7.cloned.1.call-start = ((), (), s32[]{:S(2)}) async-start(), calls=%async_computation.12 | async-start | bytes 7864320 | tf_op jit(solution)/shard_map/reduce_scatter | solution.py:443
  212.6 15.6 %collective-permute-start.14 = (bf16[128,2048]{1,0:T(8,128)(2,1)}, bf16[128,2048]{1,0:T(8,128)(2,1)}, u32[]{:S(2)}, u32[]{:S(2)}) collective-permute-start(bf16[128,2048]{1,0:T(8,128)(2,1)} %get-tuple-element.33), channel_id=1, source_target_pairs={{0,4},{4,0},{1,5},{5,1},{2,6},{6,2},{3,7},{7,3},{8,12},{12,8},{9,1... | collective-permute-start | bytes 1572872 | tf_op jit(solution)/shard_map/ppermute | solution.py:323
  216.6 14.3 %collective-permute-start.16 = (bf16[128,2048]{1,0:T(8,128)(2,1)}, bf16[128,2048]{1,0:T(8,128)(2,1)}, u32[]{:S(2)}, u32[]{:S(2)}) collective-permute-start(bf16[128,2048]{1,0:T(8,128)(2,1)} %add_convert_fusion.3), channel_id=1, source_target_pairs={{0,8},{8,0},{1,9},{9,1},{2,10},{10,2},{3,11},{11,3},{4,12},{12,4},... | collective-permute-start | bytes 1572872 | tf_op jit(solution)/shard_map/ppermute | solution.py:323
  224.4 19.4 %collective-permute-start.26 = (bf16[128,4,128]{2,0,1:T(8,128)(2,1)S(1)}, bf16[128,4,128]{2,0,1:T(8,128)(2,1)S(1)}, u32[]{:S(2)}, u32[]{:S(2)}) collective-permute-start(bf16[128,4,128]{2,0,1:T(8,128)(2,1)S(1)} %bitcast.170), channel_id=1, source_target_pairs={{0,4},{4,0},{1,5},{5,1},{2,6},{6,2},{3,7},{7,3},{8,12},{12,8},{9,1... | collective-permute-start | bytes 393224 | tf_op jit(solution)/shard_map/ppermute | solution.py:323
  227.5 22.6 %collective-permute-start.24 = (bf16[128,4,128]{2,0,1:T(8,128)(2,1)}, bf16[128,4,128]{2,0,1:T(8,128)(2,1)}, u32[]{:S(2)}, u32[]{:S(2)}) collective-permute-start(bf16[128,4,128]{2,0,1:T(8,128)(2,1)} %bitcast.142), channel_id=1, source_target_pairs={{0,4},{4,0},{1,5},{5,1},{2,6},{6,2},{3,7},{7,3},{8,12},{12,8},{9,1... | collective-permute-start | bytes 393224 | tf_op jit(solution)/shard_map/ppermute | solution.py:323
  228.1 25.4 %collective-permute-start.28 = (bf16[128,4,128]{2,0,1:T(8,128)(2,1)S(1)}, bf16[128,4,128]{2,0,1:T(8,128)(2,1)}, u32[]{:S(2)}, u32[]{:S(2)}) collective-permute-start(bf16[128,4,128]{2,0,1:T(8,128)(2,1)S(1)} %bitcast.169), channel_id=1, source_target_pairs={{0,4},{4,0},{1,5},{5,1},{2,6},{6,2},{3,7},{7,3},{8,12},{12,8},{9,1... | collective-permute-start | bytes 393224 | tf_op jit(solution)/shard_map/ppermute | solution.py:323
  233.4 25.1 %collective-permute-start.25 = (bf16[128,3072]{1,0:T(8,128)(2,1)}, bf16[128,3072]{1,0:T(8,128)(2,1)}, u32[]{:S(2)}, u32[]{:S(2)}) collective-permute-start(bf16[128,3072]{1,0:T(8,128)(2,1)} %pad_maximum_fusion.3), channel_id=1, source_target_pairs={{0,4},{4,0},{1,5},{5,1},{2,6},{6,2},{3,7},{7,3},{8,12},{12,8},{9,1... | collective-permute-start | bytes 2359304 | tf_op jit(solution)/shard_map/ppermute | solution.py:323
  240.4 14.8 %collective-permute-start.29 = (bf16[128,1024]{1,0:T(8,128)(2,1)}, bf16[128,1024]{1,0:T(8,128)(2,1)}, u32[]{:S(2)}, u32[]{:S(2)}) collective-permute-start(bf16[128,1024]{1,0:T(8,128)(2,1)} %get-tuple-element.146), channel_id=1, source_target_pairs={{0,4},{4,0},{1,5},{5,1},{2,6},{6,2},{3,7},{7,3},{8,12},{12,8},{9,1... | collective-permute-start | bytes 786440 | tf_op jit(solution)/shard_map/ppermute | solution.py:323
  244.5 12.4 %collective-permute-start.27 = (bf16[128,1024]{1,0:T(8,128)(2,1)}, bf16[128,1024]{1,0:T(8,128)(2,1)}, u32[]{:S(2)}, u32[]{:S(2)}) collective-permute-start(bf16[128,1024]{1,0:T(8,128)(2,1)} %fusion.39), channel_id=1, source_target_pairs={{0,4},{4,0},{1,5},{5,1},{2,6},{6,2},{3,7},{7,3},{8,12},{12,8},{9,1... | collective-permute-start | bytes 786440 | tf_op jit(solution)/shard_map/ppermute | solution.py:323
  263.9 183.3 %reduce-scatter.15.cloned.1.call-start = ((), (), s32[]{:S(2)}) async-start(), calls=%async_computation.16 | async-start | bytes 2359296 | tf_op jit(solution)/shard_map/reduce_scatter | solution.py:443
  338.4 26.0 %all-to-all-start.3 = ((bf16[8,4,32,384]{3,2,1,0:T(8,128)(2,1)}), bf16[8,4,32,384]{3,2,1,0:T(8,128)(2,1)}, u32[]{:S(2)}, u32[]{:S(2)}) async-start(bf16[8,4,32,384]{3,2,1,0:T(8,128)(2,1)} %add_convert_fusion), calls=%async_computation.3 | async-start | bytes 1572864 | tf_op jit(solution)/shard_map/all_to_all | solution.py:353
  342.7 114.0 %reduce-scatter.9.cloned.1.call-start = ((), (), s32[]{:S(2)}) async-start(), calls=%async_computation.13 | async-start | bytes 3932160 | tf_op jit(solution)/shard_map/reduce_scatter | solution.py:443
  371.4 26.8 %all-to-all-start.4 = ((bf16[16,2,32,384]{3,2,1,0:T(8,128)(2,1)}), bf16[16,2,32,384]{3,2,1,0:T(8,128)(2,1)}, u32[]{:S(2)}, u32[]{:S(2)}) async-start(bf16[16,2,32,384]{3,2,1,0:T(8,128)(2,1)} %fusion.5), calls=%async_computation.4 | async-start | bytes 1572864 | tf_op jit(solution)/shard_map/all_to_all | solution.py:353
  400.5 50.4 %all-to-all-start.5 = ((bf16[16,2,32,384]{3,2,1,0:T(8,128)(2,1)}), bf16[16,2,32,384]{3,2,1,0:T(8,128)(2,1)}, u32[]{:S(2)}, u32[]{:S(2)}) async-start(bf16[16,2,32,384]{3,2,1,0:T(8,128)(2,1)} %broadcast_in_dim.133), calls=%async_computation.5 | async-start | bytes 1572864 | tf_op jit(solution)/shard_map/all_to_all | solution.py:345
  404.8 66.8 %reduce-scatter.17.cloned.1.call-start = ((), (), s32[]{:S(2)}) async-start(), calls=%async_computation.17 | async-start | bytes 983040 | tf_op jit(solution)/shard_map/reduce_scatter | solution.py:443
  407.0 11.7 %collective-permute-start.8 = (bf16[1,32,1024]{2,1,0:T(8,128)(2,1)S(1)}, bf16[1,32,1024]{2,1,0:T(8,128)(2,1)S(1)}, u32[]{:S(2)}, u32[]{:S(2)}) collective-permute-start(bf16[1,32,1024]{2,1,0:T(8,128)(2,1)S(1)} %constant_dynamic-slice_fusion.20), channel_id=1, source_target_pairs={{0,1},{1,0},{2,3},{3,2},{4,5},{5,4},{6,7},{7,6},{8,9},{9,8},{10,11... | collective-permute-start | bytes 196616 | tf_op jit(solution)/shard_map/ppermute | solution.py:333
  418.7 9.5 %collective-permute-start.9 = (bf16[1,32,1024]{2,1,0:T(8,128)(2,1)S(1)}, bf16[1,32,1024]{2,1,0:T(8,128)(2,1)S(1)}, u32[]{:S(2)}, u32[]{:S(2)}) collective-permute-start(bf16[1,32,1024]{2,1,0:T(8,128)(2,1)S(1)} %get-tuple-element.180), channel_id=1, source_target_pairs={{0,2},{1,3},{2,0},{3,1},{4,6},{5,7},{6,4},{7,5},{8,10},{9,11},{10,... | collective-permute-start | bytes 196616 | tf_op jit(solution)/shard_map/ppermute | solution.py:333
  447.3 55.3 %reduce-scatter.11.cloned.1.call-start = ((), (), s32[]{:S(2)}) async-start(), calls=%async_computation.14 | async-start | bytes 1638400 | tf_op jit(solution)/shard_map/reduce_scatter | solution.py:443
  (92 other events, 576.6 us)
Sparse Core Ops, SparseCore 0:
  202.1 43.9 reduce-scatter.12
  263.7 66.3 reduce-scatter.6
  332.3 34.5 reduce-scatter.14
  369.0 53.4 reduce-scatter.8
  447.4 22.0 reduce-scatter.16
  471.6 30.8 reduce-scatter.10
